TPU v7x, 32 devices: a whole 2x2x4 slice. The times are simulated.
32 devices in a mesh: view: 2 (over core), dom: 16 (over z, y, x).
Axes of the slice: x: 2, y: 2, z: 4, core: 2. Of those that a mesh axis runs over, the one named last changes fastest.
Arguments:
- features: bfloat16 [16384, 512], P('dom'), may hold values from -6 to 6
- feat_keep: int32 [2, 512], P('view'), may hold values 0 or 1
- w_first: bfloat16 [512, 512], replicated, may hold values from -0.25 to 0.25
- w_second: bfloat16 [512, 512], replicated, may hold values from -0.25 to 0.25
- adjacency: bfloat16 [2, 1024, 128, 128], P('view', 'dom'), may hold values from 0 to 0.015625
- tile_src: int32 [2, 128, 8], P('view', 'dom'), may hold values from 0 to 8, as said below
- halo_rows: int32 [16, 16, 8], P('dom'), may hold values from 0 to 1023
- halo_live: int32 [16, 16], P('dom'), may hold values from 0 to 8, as said below
- neg_pick: int32 [16, 16, 8], P('dom'), may hold values from 0 to 1023
Outputs:
- node_loss: float32 [2, 16384], P('view', 'dom')
- grad_first: float32 [512, 512], replicated
- grad_second: float32 [512, 512], replicated
Inputs may be any that keep to these rules, and one draw needn't show every extreme that they name: `tile_src`: the last tile of the first block of every partition reads its last halo block. `halo_live`: some receiver gets 8 live rows from every sender.
All inputs are finite; a program needn't handle non-finite values. No bound on the sum of `feat_keep` on one device may be relied on, other than what follows from the above.
Results may differ from a plain program's by a relative error of at most 0.0015.
The roundings to bfloat16 on the way count: a program that leaves them out, or rounds other values in their place, can miss the bound.
Values may be sent and summed in bfloat16 or wider, within the bound.
No kernel may reach another device: no remote copies, remote signals or barrier semaphores. Data moves between devices by JAX's collectives and lax.ppermute only.
A program may use at most 128 MiB of HBM per device.

v0:
```python
import jax
import jax.numpy as jnp
from jax import lax
from jax.sharding import PartitionSpec as P

inv_temp = 5.0
norm_eps = 1e-06


def swapped(array, axis, distance):
    return lax.ppermute(array, axis, [(i, i ^ 1 << distance) for i in range(lax.axis_size(axis))])


def mix_blocks(ext_blocks, tiles, sources, inv_deg):
    picked = ext_blocks[sources]
    summed = jnp.einsum("ntij,ntjw->niw", tiles, picked, preferred_element_type=jnp.float32)
    own_rows = ext_blocks[: sources.shape[0]].astype(jnp.float32)
    return ((own_rows + summed) * inv_deg[:, :, None]).astype(jnp.bfloat16)


def spread_back(grad_mixed, tiles, sources, inv_deg, total_blocks):
    scaled = (grad_mixed * inv_deg[:, :, None]).astype(jnp.bfloat16)
    spread = jnp.einsum("ntij,niw->ntjw", tiles, scaled, preferred_element_type=jnp.float32)
    ext_grad = jnp.zeros((total_blocks, grad_mixed.shape[1], grad_mixed.shape[2]), jnp.float32)
    ext_grad = ext_grad.at[sources].add(spread)
    return ext_grad.at[: sources.shape[0]].add(scaled.astype(jnp.float32))


def contrast(unit, partner, negatives):
    unit_f = unit.astype(jnp.float32)
    partner_f = partner.astype(jnp.float32)
    positive = inv_temp * jnp.sum(unit_f * partner_f, axis=1)
    scores = inv_temp * jnp.dot(unit, negatives.T, preferred_element_type=jnp.float32)
    expo = jnp.exp(scores)
    total = jnp.exp(positive) + jnp.sum(expo, axis=1)
    node_loss = jnp.log(total) - positive
    prob = (expo / total[:, None]).astype(jnp.bfloat16)
    own_share = jnp.exp(positive) / total
    share_less = own_share - 1.0
    g_anchor = inv_temp * (
        share_less[:, None] * partner_f
        + jnp.dot(prob, negatives, preferred_element_type=jnp.float32)
    )
    g_partner = inv_temp * share_less[:, None] * unit_f
    g_neg = inv_temp * jnp.dot(prob.T, unit, preferred_element_type=jnp.float32)
    return (node_loss, g_anchor, g_partner, g_neg, share_less)


def per_device(
    features, feat_keep, w_first, w_second, adjacency, tile_src, halo_rows, halo_live, neg_pick
):
    row_count, feat_width = features.shape
    hid_width = w_first.shape[1]
    block_rows = adjacency.shape[2]
    block_count = tile_src.shape[1]
    tile_count = tile_src.shape[2]
    part_count = lax.axis_size("dom")
    slot_cap = halo_rows.shape[2]
    neg_count = neg_pick.shape[2]
    tiles = adjacency[0].reshape(block_count, tile_count, block_rows, block_rows)
    sources = tile_src[0]
    inv_deg = 1.0 / (1.0 + jnp.sum(tiles.astype(jnp.float32), axis=(1, 3)))
    keep_cols = feat_keep[0].astype(jnp.bfloat16)
    send_rows = halo_rows[0]
    live_slots = lax.broadcasted_iota(jnp.int32, (part_count, slot_cap), 1) < halo_live[0][:, None]
    live_bf = live_slots.astype(jnp.bfloat16)[:, :, None]
    masked = features * keep_cols
    outgoing = masked[send_rows] * live_bf
    incoming = lax.all_to_all(outgoing, "dom", split_axis=0, concat_axis=0, tiled=True).reshape(
        part_count * slot_cap, feat_width
    )
    ext_first = jnp.concatenate([masked, incoming], 0).reshape(-1, block_rows, feat_width)
    mixed_first = mix_blocks(ext_first, tiles, sources, inv_deg).reshape(row_count, feat_width)
    pre_act = jnp.dot(mixed_first, w_first, preferred_element_type=jnp.float32)
    hidden = jnp.maximum(pre_act, 0.0).astype(jnp.bfloat16)
    hidden_out = hidden[send_rows] * live_bf
    hidden_in = lax.all_to_all(hidden_out, "dom", split_axis=0, concat_axis=0, tiled=True).reshape(
        part_count * slot_cap, hid_width
    )
    ext_second = jnp.concatenate([hidden, hidden_in], 0).reshape(-1, block_rows, hid_width)
    mixed_second = mix_blocks(ext_second, tiles, sources, inv_deg).reshape(row_count, hid_width)
    projected = jnp.dot(mixed_second, w_second, preferred_element_type=jnp.float32)
    inv_norm = lax.rsqrt(jnp.sum(projected * projected, axis=1, keepdims=True) + norm_eps)
    normed = projected * inv_norm
    unit = normed.astype(jnp.bfloat16)
    partner = swapped(unit, "view", 0)
    pick_rows = neg_pick[0].reshape(-1)
    neg_out = partner[neg_pick[0]]
    negatives = lax.all_to_all(neg_out, "dom", split_axis=0, concat_axis=0, tiled=True).reshape(
        part_count * neg_count, hid_width
    )
    node_loss, g_anchor, g_partner, g_neg, share_less = contrast(unit, partner, negatives)
    returned = lax.all_to_all(
        g_neg.reshape(part_count, neg_count, hid_width),
        "dom",
        split_axis=0,
        concat_axis=0,
        tiled=True,
    )
    g_partner = g_partner.at[pick_rows].add(returned.reshape(-1, hid_width))
    g_emb = g_anchor + swapped(g_partner, "view", 0)
    inner = jnp.sum(normed * g_emb, axis=1, keepdims=True)
    g_proj = ((g_emb - normed * inner) * inv_norm).astype(jnp.bfloat16)
    grad_second = jnp.einsum("ih,ik->hk", mixed_second, g_proj, preferred_element_type=jnp.float32)
    g_mixed = jnp.einsum("ik,hk->ih", g_proj, w_second, preferred_element_type=jnp.float32)
    ext_grad = spread_back(
        g_mixed.reshape(block_count, block_rows, hid_width),
        tiles,
        sources,
        inv_deg,
        ext_second.shape[0],
    )
    flat_grad = ext_grad.reshape(-1, hid_width)
    halo_grad = flat_grad[row_count:].reshape(part_count, slot_cap, hid_width)
    back_grad = lax.all_to_all(
        halo_grad.astype(jnp.bfloat16), "dom", split_axis=0, concat_axis=0, tiled=True
    ).astype(halo_grad.dtype)
    back_grad = back_grad * live_slots.astype(jnp.float32)[:, :, None]
    g_hidden = flat_grad[:row_count].at[send_rows.reshape(-1)].add(back_grad.reshape(-1, hid_width))
    g_pre = jnp.where(pre_act > 0, g_hidden, 0.0).astype(jnp.bfloat16)
    grad_first = jnp.einsum("if,ih->fh", mixed_first, g_pre, preferred_element_type=jnp.float32)
    summed = lax.psum((grad_first, grad_second), ("view", "dom"))
    return (node_loss[None, :], summed[0], summed[1])


def solution(mesh):
    placed = (
        P("dom", None),
        P("view", None),
        P(),
        P(),
        P("view", "dom", None, None),
        P("view", "dom", None),
        P("dom", None, None),
        P("dom", None),
        P("dom", None, None),
    )
    return jax.shard_map(
        per_device,
        mesh=mesh,
        in_specs=placed,
        out_specs=(P("view", "dom"), P(), P()),
        check_vma=False,
    )
```

profile of v0, /device:TPU:0, one launch (start us, length us, event | category | flops | bytes accessed | tf_op | source)
XLA Modules:
  0.0 339.7 jit_solution(16240361134284853910)
XLA Ops:
  7.2 0.9 convert_reduce_fusion.1
  8.1 0.7 compare_select_fusion.2
  8.8 0.1 reshape.337
  8.9 1.3 fusion.26
  10.2 2.3 broadcast_multiply_fusion
  12.5 2.2 gather_fusion
  14.7 0.7 bitcast_multiply_fusion.1
  15.5 8.3 %all-to-all-start = ((bf16[16,8,512]{2,1,0:T(8,128)(2,1)}), bf16[16,8,512]{2,1,0:T(8,128)(2,1)S(1)}, u32[]{:S(2)}, u32[]{:S(2)}) async-start(bf16[16,8,512]{2,1,0:T(8,128)(2,1)} %bitcast_multiply_fusion.1), calls=%async_computation | async-start | bytes 262144 | tf_op jit(solution)/shard_map/all_to_all | solution.py:69
  23.9 0.1 reshape.345
  23.9 0.6 convert_reduce_fusion
  24.6 7.0 %all-to-all-done = bf16[16,8,512]{2,1,0:T(8,128)(2,1)S(1)} async-done(((bf16[16,8,512]{2,1,0:T(8,128)(2,1)}), bf16[16,8,512]{2,1,0:T(8,128)(2,1)S(1)}, u32[]{:S(2)}, u32[]{:S(2)}) %all-to-all-start) | async-done | bytes 131104 | tf_op jit(solution)/shard_map/all_to_all | solution.py:69
  31.6 1.3 pad_maximum_fusion
  33.0 5.5 %gather_fusion.1 = bf16[64,128,512]{2,1,0:T(8,128)(2,1)} fusion(bf16[9,128,512]{2,1,0:T(8,128)(2,1)S(1)} %bitcast.105, s32[1024]{0:T(1024)S(1)} %pad_clamp_fusion.1), kind=kCustom, calls=%fused_computation.1 | custom fusion | bytes 16777472 | tf_op jit(solution)/shard_map/gather | solution.py:15
  38.5 5.4 %fusion.7 = bf16[8,128,512]{2,1,0:T(8,128)(2,1)S(1)} fusion(bf16[8,128,512]{2,1,0:T(8,128)(2,1)S(1)} %bitcast.114, bf16[8,8,128,128]{3,2,1,0:T(8,128)(2,1)} %bitcast.107, bf16[8,8,128,512]{3,2,1,0:T(8,128)(2,1)} %bitcast.111, f32[8,128]{1,0:T(8,128)S(1)} %add_divide_fusion), kind=kOutput, calls=%fused_computation.23 | convolution fusion | flops 1075838976 | bytes 12587008 | tf_op jit(solution)/shard_map/ntij,ntjw->niw/dot_general | solution.py:16
  43.9 2.1 maximum_convert_fusion
  45.9 0.8 gather_fusion.2
  46.8 0.1 bitcast_multiply_fusion
  46.9 10.4 %all_to_all.25 = bf16[16,8,512]{2,1,0:T(8,128)(2,1)S(1)} all-to-all(bf16[16,8,512]{2,1,0:T(8,128)(2,1)S(1)} %bitcast_multiply_fusion), channel_id=1, replica_groups=mesh['view'=2,'dom'=16] {'dom'}, dimensions={0} | all-to-all | bytes 262144 | tf_op jit(solution)/shard_map/all_to_all | solution.py:77
  57.3 0.1 pad_maximum_fusion.1
  57.3 5.5 %gather_fusion.3 = bf16[64,128,512]{2,1,0:T(8,128)(2,1)} fusion(bf16[9,128,512]{2,1,0:T(8,128)(2,1)S(1)} %bitcast.104, s32[1024]{0:T(1024)S(1)} %pad_clamp_fusion.1), kind=kCustom, calls=%fused_computation.3 | custom fusion | bytes 16777472 | tf_op jit(solution)/shard_map/gather | solution.py:15
  62.9 5.3 %fusion.5 = bf16[8,128,512]{2,1,0:T(8,128)(2,1)S(1)} fusion(bf16[8,128,512]{2,1,0:T(8,128)(2,1)S(1)} %bitcast.115, bf16[8,8,128,128]{3,2,1,0:T(8,128)(2,1)} %bitcast.108, bf16[8,8,128,512]{3,2,1,0:T(8,128)(2,1)} %bitcast.110, f32[8,128]{1,0:T(8,128)S(1)} %add_divide_fusion), kind=kOutput, calls=%fused_computation.20 | convolution fusion | flops 1075838976 | bytes 12587008 | tf_op jit(solution)/shard_map/ntij,ntjw->niw/dot_general | solution.py:16
  68.2 0.8 multiply_reduce_fusion.1
  69.0 1.2 multiply_convert_fusion.2
  70.3 0.1 reshape.369
  70.4 2.8 collective-permute-done
  73.2 2.3 copy.31
  75.5 2.9 gather_fusion.4
  78.4 3.5 %all-to-all-start.2 = ((bf16[16,8,512]{2,1,0:T(8,128)(2,1)}), bf16[16,8,512]{2,1,0:T(8,128)(2,1)S(1)}, u32[]{:S(2)}, u32[]{:S(2)}) async-start(bf16[16,8,512]{2,1,0:T(8,128)(2,1)} %bitcast.25), calls=%async_computation.2 | async-start | bytes 262144 | tf_op jit(solution)/shard_map/all_to_all | solution.py:89
  82.0 0.7 reshape_squeeze.10
  82.6 1.6 fusion
  84.2 5.7 %all-to-all-done.2 = bf16[16,8,512]{2,1,0:T(8,128)(2,1)S(1)} async-done(((bf16[16,8,512]{2,1,0:T(8,128)(2,1)}), bf16[16,8,512]{2,1,0:T(8,128)(2,1)S(1)}, u32[]{:S(2)}, u32[]{:S(2)}) %all-to-all-start.2) | async-done | bytes 131104 | tf_op jit(solution)/shard_map/all_to_all | solution.py:89
  89.9 1.6 fusion.31
  91.5 0.6 broadcast_multiply_fusion.1
  92.1 2.4 fusion.9
  94.5 3.7 %all-to-all-start.3 = ((f32[16,8,512]{2,1,0:T(8,128)}), f32[16,8,512]{2,1,0:T(8,128)S(1)}, u32[]{:S(2)}, u32[]{:S(2)}) async-start(f32[16,8,512]{2,1,0:T(8,128)} %fusion.9), calls=%async_computation.3 | async-start | bytes 524288 | tf_op jit(solution)/shard_map/all_to_all | solution.py:93
  98.2 1.2 fusion.28
  99.4 2.3 convert_multiply_fusion.2
  101.7 2.9 copy.33
  104.6 2.8 all-to-all-done.3
  107.4 4.4 %scatter_custom_fusion = f32[1024,512]{1,0:T(8,128)} fusion(f32[1024,512]{1,0:T(8,128)} %copy.33, s32[128]{0:T(128)} %fusion.28, f32[16,8,512]{2,1,0:T(8,128)S(1)} %all-to-all-done.3), kind=kCustom, calls=%fused_computation.45 | custom fusion | flops 65536 | bytes 2359296 | tf_op jit(solution)/shard_map/scatter-add | solution.py:100
  111.7 2.9 copy.34
  114.7 0.1 reshape_squeeze.11
  114.8 4.3 %collective-permute-done.1 = f32[1024,512]{0,1:T(8,128)} collective-permute-done((f32[1024,512]{0,1:T(8,128)}, f32[1024,512]{0,1:T(8,128)}, u32[]{:S(2)}, u32[]{:S(2)}) %collective-permute-start.1) | collective-permute-done | bytes 2097184 | tf_op jit(solution)/shard_map/ppermute | solution.py:11
  119.1 2.6 multiply_reduce_fusion
  121.8 0.5 multiply_convert_fusion.1
  122.3 1.0 copy-done.9
  123.3 0.8 fusion.32
  124.0 1.4 copy-done.4
  125.4 8.2 %convolution_bitcast_fusion = f32[8,8,128,512]{2,3,1,0:T(8,128)} fusion(bf16[8,8,128,128]{3,2,1,0:T(8,128)(2,1)S(1)} %bitcast.109, f32[8,128,512]{2,1,0:T(8,128)S(1)} %bitcast.112, f32[8,128]{1,0:T(8,128)S(1)} %add_divide_fusion), kind=kOutput, calls=%fused_computation.8 | convolution fusion | flops 1074790400 | bytes 20975616 | tf_op jit(solution)/shard_map/ntij,niw->ntjw/dot_general | solution.py:23
  133.6 16.5 %copy.36 = f32[8,8,128,512]{3,2,1,0:T(8,128)} copy(f32[8,8,128,512]{2,3,1,0:T(8,128)} %convolution_bitcast_fusion) | data formatting | bytes 33554432 | tf_op jit(solution)/shard_map/ntij,niw->ntjw/dot_general | solution.py:23
  150.0 0.3 broadcast_in_dim.3
  150.3 23.0 %scatter_fusion = f32[9,128,512]{2,1,0:T(8,128)S(1)} fusion(f32[9,128,512]{2,1,0:T(8,128)S(1)} %broadcast_in_dim.3, s32[64]{0:T(128)S(1)} %reshape.345, f32[64,128,512]{2,1,0:T(8,128)} %bitcast.106), kind=kCustom, calls=%fused_computation.6 | custom fusion | flops 4194304 | bytes 50331904 | tf_op jit(solution)/shard_map/scatter-add | solution.py:25
  173.4 3.2 slice_add_fusion
  176.6 0.7 fusion.19
  177.3 3.9 %all-to-all-start.4 = ((bf16[16,8,512]{2,1,0:T(8,128)(2,1)}), bf16[16,8,512]{2,1,0:T(8,128)(2,1)S(1)}, u32[]{:S(2)}, u32[]{:S(2)}) async-start(bf16[16,8,512]{2,1,0:T(8,128)(2,1)} %fusion.19), calls=%async_computation.4 | async-start | bytes 262144 | tf_op jit(solution)/shard_map/all_to_all | solution.py:115
  181.2 3.3 fusion.33
  184.6 4.4 %all-to-all-done.4 = bf16[16,8,512]{2,1,0:T(8,128)(2,1)S(1)} async-done(((bf16[16,8,512]{2,1,0:T(8,128)(2,1)}), bf16[16,8,512]{2,1,0:T(8,128)(2,1)S(1)}, u32[]{:S(2)}, u32[]{:S(2)}) %all-to-all-start.4) | async-done | bytes 131104 | tf_op jit(solution)/shard_map/all_to_all | solution.py:115
  189.0 4.3 %scatter_custom_fusion.2 = f32[1024,512]{1,0:T(8,128)} fusion(f32[1024,512]{1,0:T(8,128)} %bitcast.118, s32[128]{0:T(128)S(1)} %fusion.29, bf16[16,8,512]{2,1,0:T(8,128)(2,1)S(1)} %all-to-all-done.4, f32[16,8]{1,0:T(8,128)S(1)} %copy-done.12), kind=kCustom, calls=%fused_computation.43 | custom fusion | flops 196608 | bytes 2236416 | tf_op jit(solution)/shard_map/scatter-add | solution.py:119
  193.3 3.9 %fusion.10 = f32[512,512]{1,0:T(8,128)} fusion(bf16[1024,512]{1,0:T(8,128)(2,1)S(1)} %bitcast.117, f32[1024,512]{1,0:T(8,128)} %scatter_custom_fusion.2, f32[1024,512]{1,0:T(8,128)} %get-tuple-element.24), kind=kOutput, calls=%fused_computation.37 | convolution fusion | flops 537919488 | bytes 6291456 | tf_op jit(solution)/shard_map/if,ih->fh/dot_general | solution.py:121
  197.2 0.6 copy-done.18
  197.9 0.6 log_subtract_fusion
  198.5 131.0 %all-reduce.3.cloned.1.call-done = (f32[512,512]{1,0:T(8,128)}, f32[512,512]{1,0:T(8,128)}) async-done(((f32[512,512]{1,0:T(8,128)}, f32[512,512]{1,0:T(8,128)}), (f32[512,512]{1,0:T(8,128)}, f32[512,512]{1,0:T(8,128)})) %all-reduce.3.cloned.1.call-update) | async-done | bytes 2097168 | tf_op jit(solution)/shard_map/psum | solution.py:122
  329.5 2.4 copy.48
  331.9 1.0 copy.49
  (54 shorter events, 0.5 us)
Async XLA Ops:
  7.2 61.0 %copy-start = (bf16[512,512]{1,0:T(8,128)(2,1)S(1)}, bf16[512,512]{1,0:T(8,128)(2,1)}, u32[]{:S(2)}) copy-start(bf16[512,512]{1,0:T(8,128)(2,1)} %param.14) | copy-start | bytes 1572868
  7.2 16.7 %copy-start.19 = (s32[1,8,8]{2,1,0:T(8,128)S(1)}, s32[1,8,8]{2,1,0:T(8,128)}, u32[]{:S(2)}) copy-start(s32[1,8,8]{2,1,0:T(8,128)} %param.16) | copy-start | bytes 772
  7.2 16.8 %copy-start.2 = (bf16[1,64,128,128]{3,2,1,0:T(8,128)(2,1)S(1)}, bf16[1,64,128,128]{3,2,1,0:T(8,128)(2,1)}, u32[]{:S(2)}) copy-start(bf16[1,64,128,128]{3,2,1,0:T(8,128)(2,1)} %param.15) | copy-start | bytes 6291460
  15.5 16.1 %all-to-all-start = ((bf16[16,8,512]{2,1,0:T(8,128)(2,1)}), bf16[16,8,512]{2,1,0:T(8,128)(2,1)S(1)}, u32[]{:S(2)}, u32[]{:S(2)}) async-start(bf16[16,8,512]{2,1,0:T(8,128)(2,1)} %bitcast_multiply_fusion.1), calls=%async_computation | async-start | bytes 262144 | tf_op jit(solution)/shard_map/all_to_all | solution.py:69
  32.9 5.5 %copy-start.5 = (bf16[1024,512]{1,0:T(8,128)(2,1)S(1)}, bf16[1024,512]{1,0:T(8,128)(2,1)}, u32[]{:S(2)}) copy-start(bf16[1024,512]{1,0:T(8,128)(2,1)} %broadcast_multiply_fusion) | copy-start | bytes 3145732
  38.5 5.4 %copy-start.11 = (bf16[512,512]{1,0:T(8,128)(2,1)S(1)}, bf16[512,512]{1,0:T(8,128)(2,1)}, u32[]{:S(2)}) copy-start(bf16[512,512]{1,0:T(8,128)(2,1)} %param.13) | copy-start | bytes 1572868
  43.8 2.1 copy-start.6
  68.2 2.1 copy-start.8
  69.0 1.3 copy-start.16
  70.2 3.0 collective-permute-start
  78.4 11.5 %all-to-all-start.2 = ((bf16[16,8,512]{2,1,0:T(8,128)(2,1)}), bf16[16,8,512]{2,1,0:T(8,128)(2,1)S(1)}, u32[]{:S(2)}, u32[]{:S(2)}) async-start(bf16[16,8,512]{2,1,0:T(8,128)(2,1)} %bitcast.25), calls=%async_computation.2 | async-start | bytes 262144 | tf_op jit(solution)/shard_map/all_to_all | solution.py:89
  92.1 2.4 copy-start.14
  94.5 12.8 %all-to-all-start.3 = ((f32[16,8,512]{2,1,0:T(8,128)}), f32[16,8,512]{2,1,0:T(8,128)S(1)}, u32[]{:S(2)}, u32[]{:S(2)}) async-start(f32[16,8,512]{2,1,0:T(8,128)} %fusion.9), calls=%async_computation.3 | async-start | bytes 524288 | tf_op jit(solution)/shard_map/all_to_all | solution.py:93
  111.7 2.9 copy-start.17
  111.7 7.4 %copy-start.13 = (f32[1024]{0:T(1024)S(1)}, f32[1024]{0:T(1024)}, u32[]{:S(2)}) copy-start(f32[1024]{0:T(1024)} %get-tuple-element.18) | copy-start | bytes 12292
  111.7 7.4 %copy-start.15 = (f32[1024]{0:T(1024)S(1)}, f32[1024]{0:T(1024)}, u32[]{:S(2)}) copy-start(f32[1024]{0:T(1024)} %copy-done.14) | copy-start | bytes 12292
  114.6 4.5 %collective-permute-start.1 = (f32[1024,512]{0,1:T(8,128)}, f32[1024,512]{0,1:T(8,128)}, u32[]{:S(2)}, u32[]{:S(2)}) collective-permute-start(f32[1024,512]{0,1:T(8,128)} %copy.34), channel_id=1, source_target_pairs={{0,16},{16,0},{1,17},{17,1},{2,18},{18,2},{3,19},{19,3},{4,20},{20... | collective-permute-start | bytes 6291464 | tf_op jit(solution)/shard_map/ppermute | solution.py:11
  122.3 1.0 copy-start.9
  123.3 2.2 copy-start.3
  124.0 1.4 copy-start.4
  176.6 12.4 %copy-start.12 = (f32[16,8]{1,0:T(8,128)S(1)}, f32[16,8]{1,0:T(8,128)}, u32[]{:S(2)}) copy-start(f32[16,8]{1,0:T(8,128)} %get-tuple-element.21) | copy-start | bytes 1540
  177.3 11.7 %all-to-all-start.4 = ((bf16[16,8,512]{2,1,0:T(8,128)(2,1)}), bf16[16,8,512]{2,1,0:T(8,128)(2,1)S(1)}, u32[]{:S(2)}, u32[]{:S(2)}) async-start(bf16[16,8,512]{2,1,0:T(8,128)(2,1)} %fusion.19), calls=%async_computation.4 | async-start | bytes 262144 | tf_op jit(solution)/shard_map/all_to_all | solution.py:115
  181.2 12.1 %copy-start.7 = (bf16[8,128,512]{2,1,0:T(8,128)(2,1)S(1)}, bf16[8,128,512]{2,1,0:T(8,128)(2,1)}, u32[]{:S(2)}) copy-start(bf16[8,128,512]{2,1,0:T(8,128)(2,1)} %copy-done.6) | copy-start | bytes 3145732
  181.2 148.3 %all-reduce.3.cloned.1.call-start = ((), (), s32[]{:S(2)}) async-start(), calls=%async_computation.5 | async-start | bytes 4194304 | tf_op jit(solution)/shard_map/psum | solution.py:122
  197.2 0.7 copy-start.18
  329.5 2.4 copy-start.10
  329.5 3.4 copy-start.1
Sparse Core Ops, SparseCore 0:
  197.3 132.1 all-reduce.2
where the time goes:
time: 341 us; the launch traced here: 340 us
  waiting for transfers between devices  158 us (46%)
  other arithmetic  50.9 us (15%)
  local copies, waits for them, and re-layouts  50.3 us (15%)
  matrix products  36.3 us (11%)
  starting transfers between devices  19.5 us (6%)
  between operations  14.4 us (4%)
  blocking collectives  10.4 us (3%)
    psum x1, waiting for transfers between devices, per_device(): summed = lax.psum((grad_first, grad_second), ('view', 'dom'))  131 us
    scatter-add x1, other arithmetic, spread_back(): ext_grad = ext_grad.at[sources].add(spread)  23 us
    dot_general x1, local copies, waits for them, and re-layouts, spread_back(): jnp.einsum('ntij,niw->ntjw', tiles, scaled, preferred_element_type=jnp.fl...  16.5 us
    gather x2, local copies, waits for them, and re-layouts, mix_blocks(): picked = ext_blocks[sources]  11.1 us
    dot_general x2, matrix products, mix_blocks(): jnp.einsum('ntij,ntjw->niw', tiles, picked, preferred_element_type=jnp.fl...  10.7 us
    all_to_all x1, blocking collectives, per_device(): lax.all_to_all(hidden_out, 'dom', split_axis=0, concat_axis=0, tiled=True)  10.4 us
    all_to_all x1, starting transfers between devices, per_device(): lax.all_to_all(outgoing, 'dom', split_axis=0, concat_axis=0, tiled=True)  8.34 us
    dot_general x1, matrix products, spread_back(): jnp.einsum('ntij,niw->ntjw', tiles, scaled, preferred_element_type=jnp.fl...  8.17 us
  transfers between devices with their start and end apart: 7, of which 7 were waited for; matrix products, arithmetic and copies ran while one was open for 4% of the time, Pallas kernels for 0%

commit v1 on v0

--- a/solution.py
+++ b/solution.py
@@ -2,9 +2,16 @@
 import jax.numpy as jnp
 from jax import lax
 from jax.sharding import PartitionSpec as P
+from jax.lax import psum
 
 inv_temp = 5.0
 norm_eps = 1e-06
+
+
+def derive_task(a0):
+    for j in ("dom", "view"):
+        a0 = psum(a0, axis_name=j)
+    return a0
 
 
 def swapped(array, axis, distance):
@@ -119,7 +126,7 @@
     g_hidden = flat_grad[:row_count].at[send_rows.reshape(-1)].add(back_grad.reshape(-1, hid_width))
     g_pre = jnp.where(pre_act > 0, g_hidden, 0.0).astype(jnp.bfloat16)
     grad_first = jnp.einsum("if,ih->fh", mixed_first, g_pre, preferred_element_type=jnp.float32)
-    summed = lax.psum((grad_first, grad_second), ("view", "dom"))
+    summed = derive_task((grad_first, grad_second))
     return (node_loss[None, :], summed[0], summed[1])
 
 

time: 341 us -> 356 us (1.044)
  waiting for transfers between devices: 158 us -> 174 us
    psum x1 -> x2, waiting for transfers between devices: 131 us -> 147 us  [derive_task(): a0 = psum(a0, axis_name=j)]
  transfers between devices with their start and end apart: 7 -> 8, of which waited for: 7 -> 8; matrix products, arithmetic and copies ran while one was open for 4% -> 4% of each run, Pallas kernels for 0% -> 0%
where the time goes in v1:
time: 356 us; the launch traced here: 355 us
  waiting for transfers between devices  174 us (49%)
  other arithmetic  50.9 us (14%)
  local copies, waits for them, and re-layouts  49.6 us (14%)
  matrix products  36.3 us (10%)
  starting transfers between devices  19.6 us (6%)
  between operations  14.4 us (4%)
  blocking collectives  10.4 us (3%)
    psum x2, waiting for transfers between devices, derive_task(): a0 = psum(a0, axis_name=j)  147 us
    scatter-add x1, other arithmetic, spread_back(): ext_grad = ext_grad.at[sources].add(spread)  23 us
    dot_general x1, local copies, waits for them, and re-layouts, spread_back(): jnp.einsum('ntij,niw->ntjw', tiles, scaled, preferred_element_type=jnp.fl...  16.5 us
    gather x2, local copies, waits for them, and re-layouts, mix_blocks(): picked = ext_blocks[sources]  11 us
    dot_general x2, matrix products, mix_blocks(): jnp.einsum('ntij,ntjw->niw', tiles, picked, preferred_element_type=jnp.fl...  10.6 us
    all_to_all x1, blocking collectives, per_device(): lax.all_to_all(hidden_out, 'dom', split_axis=0, concat_axis=0, tiled=True)  10.4 us
    all_to_all x1, starting transfers between devices, per_device(): lax.all_to_all(outgoing, 'dom', split_axis=0, concat_axis=0, tiled=True)  8.34 us
    dot_general x1, matrix products, spread_back(): jnp.einsum('ntij,niw->ntjw', tiles, scaled, preferred_element_type=jnp.fl...  8.19 us
  transfers between devices with their start and end apart: 8, of which 8 were waited for; matrix products, arithmetic and copies ran while one was open for 4% of the time, Pallas kernels for 0%

profile of v1, /device:TPU:0, one launch (start us, length us, event | category | flops | bytes accessed | tf_op | source)
XLA Modules:
  0.0 354.8 jit_solution(3851825764110285840)
XLA Ops:
  7.2 0.9 convert_reduce_fusion.1
  8.1 0.7 compare_select_fusion.2
  8.8 0.1 reshape.337
  8.9 1.3 fusion.26
  10.2 2.3 broadcast_multiply_fusion
  12.5 2.2 gather_fusion
  14.7 0.7 bitcast_multiply_fusion.1
  15.5 8.3 %all-to-all-start = ((bf16[16,8,512]{2,1,0:T(8,128)(2,1)}), bf16[16,8,512]{2,1,0:T(8,128)(2,1)S(1)}, u32[]{:S(2)}, u32[]{:S(2)}) async-start(bf16[16,8,512]{2,1,0:T(8,128)(2,1)} %bitcast_multiply_fusion.1), calls=%async_computation | async-start | bytes 262144 | tf_op jit(solution)/shard_map/all_to_all | solution.py:76
  23.9 0.1 reshape.345
  23.9 0.6 convert_reduce_fusion
  24.6 7.0 %all-to-all-done = bf16[16,8,512]{2,1,0:T(8,128)(2,1)S(1)} async-done(((bf16[16,8,512]{2,1,0:T(8,128)(2,1)}), bf16[16,8,512]{2,1,0:T(8,128)(2,1)S(1)}, u32[]{:S(2)}, u32[]{:S(2)}) %all-to-all-start) | async-done | bytes 131104 | tf_op jit(solution)/shard_map/all_to_all | solution.py:76
  31.6 1.3 pad_maximum_fusion
  33.0 5.5 %gather_fusion.1 = bf16[64,128,512]{2,1,0:T(8,128)(2,1)} fusion(bf16[9,128,512]{2,1,0:T(8,128)(2,1)S(1)} %bitcast.105, s32[1024]{0:T(1024)S(1)} %pad_clamp_fusion.1), kind=kCustom, calls=%fused_computation.1 | custom fusion | bytes 16777472 | tf_op jit(solution)/shard_map/gather | solution.py:22
  38.5 5.3 %fusion.7 = bf16[8,128,512]{2,1,0:T(8,128)(2,1)S(1)} fusion(bf16[8,128,512]{2,1,0:T(8,128)(2,1)S(1)} %bitcast.114, bf16[8,8,128,128]{3,2,1,0:T(8,128)(2,1)} %bitcast.107, bf16[8,8,128,512]{3,2,1,0:T(8,128)(2,1)} %bitcast.111, f32[8,128]{1,0:T(8,128)S(1)} %add_divide_fusion), kind=kOutput, calls=%fused_computation.23 | convolution fusion | flops 1075838976 | bytes 12587008 | tf_op jit(solution)/shard_map/ntij,ntjw->niw/dot_general | solution.py:23
  43.8 2.0 maximum_convert_fusion
  45.9 0.8 gather_fusion.2
  46.7 0.1 bitcast_multiply_fusion
  46.8 10.4 %all_to_all.25 = bf16[16,8,512]{2,1,0:T(8,128)(2,1)S(1)} all-to-all(bf16[16,8,512]{2,1,0:T(8,128)(2,1)S(1)} %bitcast_multiply_fusion), channel_id=1, replica_groups=mesh['view'=2,'dom'=16] {'dom'}, dimensions={0} | all-to-all | bytes 262144 | tf_op jit(solution)/shard_map/all_to_all | solution.py:84
  57.2 0.1 pad_maximum_fusion.1
  57.3 5.5 %gather_fusion.3 = bf16[64,128,512]{2,1,0:T(8,128)(2,1)} fusion(bf16[9,128,512]{2,1,0:T(8,128)(2,1)S(1)} %bitcast.104, s32[1024]{0:T(1024)S(1)} %pad_clamp_fusion.1), kind=kCustom, calls=%fused_computation.3 | custom fusion | bytes 16777472 | tf_op jit(solution)/shard_map/gather | solution.py:22
  62.8 5.3 %fusion.5 = bf16[8,128,512]{2,1,0:T(8,128)(2,1)S(1)} fusion(bf16[8,128,512]{2,1,0:T(8,128)(2,1)S(1)} %bitcast.115, bf16[8,8,128,128]{3,2,1,0:T(8,128)(2,1)} %bitcast.108, bf16[8,8,128,512]{3,2,1,0:T(8,128)(2,1)} %bitcast.110, f32[8,128]{1,0:T(8,128)S(1)} %add_divide_fusion), kind=kOutput, calls=%fused_computation.20 | convolution fusion | flops 1075838976 | bytes 12587008 | tf_op jit(solution)/shard_map/ntij,ntjw->niw/dot_general | solution.py:23
  68.1 0.8 multiply_reduce_fusion.1
  69.0 1.2 multiply_convert_fusion.2
  70.3 0.1 reshape.369
  70.4 2.8 collective-permute-done
  73.2 2.3 copy.31
  75.5 2.9 gather_fusion.4
  78.4 3.5 all-to-all-start.2
  81.9 0.7 reshape_squeeze.10
  82.6 1.6 fusion
  84.2 5.7 %all-to-all-done.2 = bf16[16,8,512]{2,1,0:T(8,128)(2,1)S(1)} async-done(((bf16[16,8,512]{2,1,0:T(8,128)(2,1)}), bf16[16,8,512]{2,1,0:T(8,128)(2,1)S(1)}, u32[]{:S(2)}, u32[]{:S(2)}) %all-to-all-start.2) | async-done | bytes 131104 | tf_op jit(solution)/shard_map/all_to_all | solution.py:96
  89.9 1.6 fusion.31
  91.4 0.6 broadcast_multiply_fusion.1
  92.0 2.4 fusion.9
  94.5 3.7 %all-to-all-start.3 = ((f32[16,8,512]{2,1,0:T(8,128)}), f32[16,8,512]{2,1,0:T(8,128)S(1)}, u32[]{:S(2)}, u32[]{:S(2)}) async-start(f32[16,8,512]{2,1,0:T(8,128)} %fusion.9), calls=%async_computation.3 | async-start | bytes 524288 | tf_op jit(solution)/shard_map/all_to_all | solution.py:100
  98.2 1.2 fusion.28
  99.4 2.3 convert_multiply_fusion.2
  101.6 2.9 copy.33
  104.6 2.7 all-to-all-done.3
  107.3 4.3 %scatter_custom_fusion = f32[1024,512]{1,0:T(8,128)} fusion(f32[1024,512]{1,0:T(8,128)} %copy.33, s32[128]{0:T(128)} %fusion.28, f32[16,8,512]{2,1,0:T(8,128)S(1)} %all-to-all-done.3), kind=kCustom, calls=%fused_computation.45 | custom fusion | flops 65536 | bytes 2359296 | tf_op jit(solution)/shard_map/scatter-add | solution.py:107
  111.7 2.9 copy.34
  114.7 0.1 reshape_squeeze.11
  114.8 4.3 %collective-permute-done.1 = f32[1024,512]{0,1:T(8,128)} collective-permute-done((f32[1024,512]{0,1:T(8,128)}, f32[1024,512]{0,1:T(8,128)}, u32[]{:S(2)}, u32[]{:S(2)}) %collective-permute-start.1) | collective-permute-done | bytes 2097184 | tf_op jit(solution)/shard_map/ppermute | solution.py:18
  119.1 2.6 multiply_reduce_fusion
  121.7 0.5 multiply_convert_fusion.1
  122.3 1.0 copy-done.9
  123.2 0.8 fusion.32
  124.0 1.4 copy-done.4
  125.4 8.2 %convolution_bitcast_fusion = f32[8,8,128,512]{2,3,1,0:T(8,128)} fusion(bf16[8,8,128,128]{3,2,1,0:T(8,128)(2,1)S(1)} %bitcast.109, f32[8,128,512]{2,1,0:T(8,128)S(1)} %bitcast.112, f32[8,128]{1,0:T(8,128)S(1)} %add_divide_fusion), kind=kOutput, calls=%fused_computation.8 | convolution fusion | flops 1074790400 | bytes 20975616 | tf_op jit(solution)/shard_map/ntij,niw->ntjw/dot_general | solution.py:30
  133.6 16.5 %copy.36 = f32[8,8,128,512]{3,2,1,0:T(8,128)} copy(f32[8,8,128,512]{2,3,1,0:T(8,128)} %convolution_bitcast_fusion) | data formatting | bytes 33554432 | tf_op jit(solution)/shard_map/ntij,niw->ntjw/dot_general | solution.py:30
  150.0 0.3 broadcast_in_dim.3
  150.3 23.0 %scatter_fusion = f32[9,128,512]{2,1,0:T(8,128)S(1)} fusion(f32[9,128,512]{2,1,0:T(8,128)S(1)} %broadcast_in_dim.3, s32[64]{0:T(128)S(1)} %reshape.345, f32[64,128,512]{2,1,0:T(8,128)} %bitcast.106), kind=kCustom, calls=%fused_computation.6 | custom fusion | flops 4194304 | bytes 50331904 | tf_op jit(solution)/shard_map/scatter-add | solution.py:32
  173.4 3.2 slice_add_fusion
  176.6 0.7 fusion.19
  177.2 3.9 %all-to-all-start.4 = ((bf16[16,8,512]{2,1,0:T(8,128)(2,1)}), bf16[16,8,512]{2,1,0:T(8,128)(2,1)S(1)}, u32[]{:S(2)}, u32[]{:S(2)}) async-start(bf16[16,8,512]{2,1,0:T(8,128)(2,1)} %fusion.19), calls=%async_computation.4 | async-start | bytes 262144 | tf_op jit(solution)/shard_map/all_to_all | solution.py:122
  181.2 3.3 fusion.33
  184.5 4.4 %all-to-all-done.4 = bf16[16,8,512]{2,1,0:T(8,128)(2,1)S(1)} async-done(((bf16[16,8,512]{2,1,0:T(8,128)(2,1)}), bf16[16,8,512]{2,1,0:T(8,128)(2,1)S(1)}, u32[]{:S(2)}, u32[]{:S(2)}) %all-to-all-start.4) | async-done | bytes 131104 | tf_op jit(solution)/shard_map/all_to_all | solution.py:122
  188.9 4.3 %scatter_custom_fusion.2 = f32[1024,512]{1,0:T(8,128)} fusion(f32[1024,512]{1,0:T(8,128)} %bitcast.118, s32[128]{0:T(128)S(1)} %fusion.29, bf16[16,8,512]{2,1,0:T(8,128)(2,1)S(1)} %all-to-all-done.4, f32[16,8]{1,0:T(8,128)S(1)} %copy-done.12), kind=kCustom, calls=%fused_computation.43 | custom fusion | flops 196608 | bytes 2236416 | tf_op jit(solution)/shard_map/scatter-add | solution.py:126
  193.2 3.9 %fusion.10 = f32[512,512]{1,0:T(8,128)} fusion(bf16[1024,512]{1,0:T(8,128)(2,1)S(1)} %bitcast.117, f32[1024,512]{1,0:T(8,128)} %scatter_custom_fusion.2, f32[1024,512]{1,0:T(8,128)} %get-tuple-element.26), kind=kOutput, calls=%fused_computation.37 | convolution fusion | flops 537919488 | bytes 6291456 | tf_op jit(solution)/shard_map/if,ih->fh/dot_general | solution.py:128
  197.2 124.4 %all-reduce.5.cloned.1.call-done = (f32[512,512]{1,0:T(8,128)}, f32[512,512]{1,0:T(8,128)}) async-done(((f32[512,512]{1,0:T(8,128)}, f32[512,512]{1,0:T(8,128)}), (f32[512,512]{1,0:T(8,128)}, f32[512,512]{1,0:T(8,128)})) %all-reduce.5.cloned.1.call-update) | async-done | bytes 2097168 | tf_op jit(solution)/shard_map/psum | solution.py:13
  321.7 0.6 log_subtract_fusion
  322.3 22.4 %all-reduce.7.cloned.1.call-done = (f32[512,512]{1,0:T(8,128)}, f32[512,512]{1,0:T(8,128)}) async-done(((f32[512,512]{1,0:T(8,128)}, f32[512,512]{1,0:T(8,128)}), (f32[512,512]{1,0:T(8,128)}, f32[512,512]{1,0:T(8,128)})) %all-reduce.7.cloned.1.call-update) | async-done | bytes 2097168 | tf_op jit(solution)/shard_map/psum | solution.py:13
  344.6 2.4 copy.50
  347.0 1.0 copy.51
  (57 shorter events, 0.6 us)
Async XLA Ops:
  7.2 61.0 %copy-start = (bf16[512,512]{1,0:T(8,128)(2,1)S(1)}, bf16[512,512]{1,0:T(8,128)(2,1)}, u32[]{:S(2)}) copy-start(bf16[512,512]{1,0:T(8,128)(2,1)} %param.14) | copy-start | bytes 1572868
  7.2 16.7 %copy-start.19 = (s32[1,8,8]{2,1,0:T(8,128)S(1)}, s32[1,8,8]{2,1,0:T(8,128)}, u32[]{:S(2)}) copy-start(s32[1,8,8]{2,1,0:T(8,128)} %param.16) | copy-start | bytes 772
  7.2 16.8 %copy-start.2 = (bf16[1,64,128,128]{3,2,1,0:T(8,128)(2,1)S(1)}, bf16[1,64,128,128]{3,2,1,0:T(8,128)(2,1)}, u32[]{:S(2)}) copy-start(bf16[1,64,128,128]{3,2,1,0:T(8,128)(2,1)} %param.15) | copy-start | bytes 6291460
  15.5 16.1 %all-to-all-start = ((bf16[16,8,512]{2,1,0:T(8,128)(2,1)}), bf16[16,8,512]{2,1,0:T(8,128)(2,1)S(1)}, u32[]{:S(2)}, u32[]{:S(2)}) async-start(bf16[16,8,512]{2,1,0:T(8,128)(2,1)} %bitcast_multiply_fusion.1), calls=%async_computation | async-start | bytes 262144 | tf_op jit(solution)/shard_map/all_to_all | solution.py:76
  32.9 5.5 %copy-start.5 = (bf16[1024,512]{1,0:T(8,128)(2,1)S(1)}, bf16[1024,512]{1,0:T(8,128)(2,1)}, u32[]{:S(2)}) copy-start(bf16[1024,512]{1,0:T(8,128)(2,1)} %broadcast_multiply_fusion) | copy-start | bytes 3145732
  38.5 5.4 %copy-start.11 = (bf16[512,512]{1,0:T(8,128)(2,1)S(1)}, bf16[512,512]{1,0:T(8,128)(2,1)}, u32[]{:S(2)}) copy-start(bf16[512,512]{1,0:T(8,128)(2,1)} %param.13) | copy-start | bytes 1572868
  43.8 2.1 copy-start.6
  68.1 2.1 copy-start.8
  68.9 1.3 copy-start.16
  70.2 3.0 collective-permute-start
  78.4 11.5 %all-to-all-start.2 = ((bf16[16,8,512]{2,1,0:T(8,128)(2,1)}), bf16[16,8,512]{2,1,0:T(8,128)(2,1)S(1)}, u32[]{:S(2)}, u32[]{:S(2)}) async-start(bf16[16,8,512]{2,1,0:T(8,128)(2,1)} %bitcast.25), calls=%async_computation.2 | async-start | bytes 262144 | tf_op jit(solution)/shard_map/all_to_all | solution.py:96
  92.0 2.4 copy-start.14
  94.5 12.8 %all-to-all-start.3 = ((f32[16,8,512]{2,1,0:T(8,128)}), f32[16,8,512]{2,1,0:T(8,128)S(1)}, u32[]{:S(2)}, u32[]{:S(2)}) async-start(f32[16,8,512]{2,1,0:T(8,128)} %fusion.9), calls=%async_computation.3 | async-start | bytes 524288 | tf_op jit(solution)/shard_map/all_to_all | solution.py:100
  111.7 2.9 copy-start.17
  111.7 7.4 %copy-start.13 = (f32[1024]{0:T(1024)S(1)}, f32[1024]{0:T(1024)}, u32[]{:S(2)}) copy-start(f32[1024]{0:T(1024)} %get-tuple-element.20) | copy-start | bytes 12292
  111.7 7.4 %copy-start.15 = (f32[1024]{0:T(1024)S(1)}, f32[1024]{0:T(1024)}, u32[]{:S(2)}) copy-start(f32[1024]{0:T(1024)} %copy-done.14) | copy-start | bytes 12292
  114.6 4.5 %collective-permute-start.1 = (f32[1024,512]{0,1:T(8,128)}, f32[1024,512]{0,1:T(8,128)}, u32[]{:S(2)}, u32[]{:S(2)}) collective-permute-start(f32[1024,512]{0,1:T(8,128)} %copy.34), channel_id=1, source_target_pairs={{0,16},{16,0},{1,17},{17,1},{2,18},{18,2},{3,19},{19,3},{4,20},{20... | collective-permute-start | bytes 6291464 | tf_op jit(solution)/shard_map/ppermute | solution.py:18
  122.2 1.0 copy-start.9
  123.2 2.2 copy-start.3
  124.0 1.4 copy-start.4
  176.6 12.4 %copy-start.12 = (f32[16,8]{1,0:T(8,128)S(1)}, f32[16,8]{1,0:T(8,128)}, u32[]{:S(2)}) copy-start(f32[16,8]{1,0:T(8,128)} %get-tuple-element.23) | copy-start | bytes 1540
  177.2 11.7 %all-to-all-start.4 = ((bf16[16,8,512]{2,1,0:T(8,128)(2,1)}), bf16[16,8,512]{2,1,0:T(8,128)(2,1)S(1)}, u32[]{:S(2)}, u32[]{:S(2)}) async-start(bf16[16,8,512]{2,1,0:T(8,128)(2,1)} %fusion.19), calls=%async_computation.4 | async-start | bytes 262144 | tf_op jit(solution)/shard_map/all_to_all | solution.py:122
  181.1 12.1 %copy-start.7 = (bf16[8,128,512]{2,1,0:T(8,128)(2,1)S(1)}, bf16[8,128,512]{2,1,0:T(8,128)(2,1)}, u32[]{:S(2)}) copy-start(bf16[8,128,512]{2,1,0:T(8,128)(2,1)} %copy-done.6) | copy-start | bytes 3145732
  181.1 140.5 %all-reduce.5.cloned.1.call-start = ((), (), s32[]{:S(2)}) async-start(), calls=%async_computation.5 | async-start | bytes 4194304 | tf_op jit(solution)/shard_map/psum | solution.py:13
  197.2 124.5 %copy-start.18 = (f32[1024]{0:T(1024)S(1)}, f32[1024]{0:T(1024)}, u32[]{:S(2)}) copy-start(f32[1024]{0:T(1024)} %get-tuple-element.22) | copy-start | bytes 12292
  197.2 147.5 %all-reduce.7.cloned.1.call-start = ((), (), s32[]{:S(2)}) async-start(), calls=%async_computation.6 | async-start | bytes 4194304 | tf_op jit(solution)/shard_map/psum | solution.py:13
  344.6 2.4 copy-start.10
  344.6 3.4 copy-start.1
Sparse Core Ops, SparseCore 0:
  197.3 124.2 all-reduce.4
  324.0 20.5 all-reduce.6
